TPU v7x, 512 devices: a whole 4x4x16 slice. The times are simulated.
512 devices in a mesh: surf: 512 (over x, z, y, core).
Axes of the slice: x: 4, y: 4, z: 16, core: 2. Of those that a mesh axis runs over, the one named last changes fastest.
Arguments:
- excitation: float32 [2, 262144, 256], P(None, 'surf'), may hold values from -6 to 6
- leaf_basis: bfloat16 [2, 131072, 512], P(None, 'surf'), may hold values from -0.1875 to 0.1875
- self_transfer: bfloat16 [3, 2, 131072, 256], P(None, None, 'surf'), may hold values from -0.1875 to 0.1875
- cross_transfer: bfloat16 [3, 2, 131072, 256], P(None, None, 'surf'), may hold values from -0.1875 to 0.1875
- out_basis: bfloat16 [2, 262144, 256], P(None, 'surf'), may hold values from -0.25 to 0.25
- near_tiles: bfloat16 [3072, 2, 128, 128], P('surf'), may hold values from -0.375 to 0.375
- near_list: int32 [512, 6, 3], replicated, may hold values from -1 to 511, as said below
Outputs:
- response: float32 [2, 262144, 256], P(None, 'surf')
Inputs may be any that keep to these rules, and one draw needn't show every extreme that they name: `near_list`: row i lists patch i's near tiles as (owner, row tile, column tile). An owner is i - 1, i or i + 1 modulo 512, or -1 for an empty slot; empty slots come last and hold 0 for both tiles. Every patch has at least one tile and some patch fills all 6 slots. From one neighbouring patch a patch lists at most 2 distinct column tiles, and some patch reaches 2.
All inputs are finite; a program needn't handle non-finite values.
Results may differ from a plain program's by a relative error of at most 0.0051.
Values may be sent and summed in bfloat16 or wider, within the bound.
A program may use at most 64 MiB of HBM per device.

v0:
```python
import jax
import jax.numpy as jnp
from jax import lax
from jax.sharding import PartitionSpec as P


def from_partner(x, axis, apart):
    return lax.ppermute(x, axis, [(i, i ^ 1 << apart) for i in range(lax.axis_size(axis))])


def extended(block, sides, width):
    for axis, dim in sides:
        count = lax.axis_size(axis)
        forward = [(i, i + 1) for i in range(count - 1)]
        forward.append((count - 1, 0))
        backward = [(target, source) for source, target in forward]
        low = lax.ppermute(
            lax.slice_in_dim(block, block.shape[dim] - width, None, axis=dim), axis, forward
        )
        high = lax.ppermute(lax.slice_in_dim(block, 0, width, axis=dim), axis, backward)
        block = jnp.concatenate([low, block, high], axis=dim)
    return block


def cmat(matrix, vector):
    real = jnp.dot(matrix[0], vector[0], preferred_element_type=jnp.float32) - jnp.dot(
        matrix[1], vector[1], preferred_element_type=jnp.float32
    )
    imag = jnp.dot(matrix[0], vector[1], preferred_element_type=jnp.float32) + jnp.dot(
        matrix[1], vector[0], preferred_element_type=jnp.float32
    )
    return jnp.stack([real, imag])


def per_device(
    excitation, leaf_basis, self_transfer, cross_transfer, out_basis, near_tiles, near_list
):
    xb = excitation.astype(jnp.bfloat16)
    rows = xb.shape[1]
    width = xb.shape[2]
    tile = near_tiles.shape[2]
    blocks = rows // tile
    coef = cmat(leaf_basis, xb).astype(jnp.bfloat16)
    for level in range(self_transfer.shape[0]):
        exchange_partner = from_partner(coef, "surf", level)
        coef = (
            cmat(self_transfer[level], coef) + cmat(cross_transfer[level], exchange_partner)
        ).astype(jnp.bfloat16)
    far = cmat(out_basis, coef)
    tile_count = lax.axis_size("surf")
    here = lax.axis_index("surf")
    mine = lax.dynamic_index_in_dim(near_list, here, 0, keepdims=False)
    owner = mine[:, 0]
    row_tile = mine[:, 1]
    column = mine[:, 2]
    valid = (owner >= 0).astype(jnp.float32)
    side = jnp.where(owner >= 0, (owner - here + 1) % tile_count, 1)
    wide = extended(xb, (("surf", 1),), rows)
    window = wide.reshape(2, 3 * blocks, tile, width)
    place = side * blocks + column
    block_ids = jnp.arange(blocks, dtype=jnp.int32)
    near = jnp.zeros((2, blocks, tile, width), jnp.float32)
    for slot in range(near_tiles.shape[0]):
        block = lax.dynamic_index_in_dim(window, place[slot], 1, keepdims=False)
        term = cmat(near_tiles[slot], block) * valid[slot]
        hit = (block_ids == row_tile[slot]).astype(jnp.float32)
        near = near + term[:, None] * hit[None, :, None, None]
    return far + near.reshape(2, rows, width)


def solution(mesh):
    placed = (
        P(None, "surf", None),
        P(None, "surf", None),
        P(None, None, "surf", None),
        P(None, None, "surf", None),
        P(None, "surf", None),
        P("surf", None, None, None),
        P(),
    )
    return jax.shard_map(
        per_device, mesh=mesh, in_specs=placed, out_specs=P(None, "surf", None), check_vma=False
    )
```

profile of v0, /device:TPU:25, one launch (start us, length us, event | category | flops | bytes accessed | tf_op | source)
XLA Modules:
  0.0 103.1 jit_solution(464429250602649360)
XLA Ops:
  0.0 1.3 %convert_element_type.58 = bf16[2,512,256]{2,1,0:T(8,128)(2,1)S(1)} convert(f32[2,512,256]{2,1,0:T(8,128)} %param.7) | non-fusion elementwise | flops 262144 | bytes 1572864 | tf_op jit(solution)/shard_map/convert_element_type | solution.py:38
  1.3 3.8 %collective-permute-start.3 = (bf16[2,512,256]{2,1,0:T(8,128)(2,1)S(1)}, bf16[2,512,256]{2,1,0:T(8,128)(2,1)}, u32[]{:S(2)}, u32[]{:S(2)}) collective-permute-start(bf16[2,512,256]{2,1,0:T(8,128)(2,1)S(1)} %convert_element_type.58), channel_id=1, source_target_pairs={{0,1},{1,2},{2,3},{3,4},{4,5},{5,6},{6,7},{7,8},{8,9},{9,10},{10,1... | collective-permute-start | bytes 1572872 | tf_op jit(solution)/shard_map/ppermute | solution.py:17
  5.1 1.9 %collective-permute-start.4 = (bf16[2,512,256]{2,1,0:T(8,128)(2,1)S(1)}, bf16[2,512,256]{2,1,0:T(8,128)(2,1)}, u32[]{:S(2)}, u32[]{:S(2)}) collective-permute-start(bf16[2,512,256]{2,1,0:T(8,128)(2,1)S(1)} %convert_element_type.58), channel_id=1, source_target_pairs={{1,0},{2,1},{3,2},{4,3},{5,4},{6,5},{7,6},{8,7},{9,8},{10,9},{11,1... | collective-permute-start | bytes 1572872 | tf_op jit(solution)/shard_map/ppermute | solution.py:20
  8.1 2.6 %collective-permute-start = (bf16[2,256,256]{2,1,0:T(8,128)(2,1)S(1)}, bf16[2,256,256]{2,1,0:T(8,128)(2,1)S(1)}, u32[]{:S(2)}, u32[]{:S(2)}) collective-permute-start(bf16[2,256,256]{2,1,0:T(8,128)(2,1)S(1)} %pad_maximum_fusion.1), channel_id=1, source_target_pairs={{0,1},{1,0},{2,3},{3,2},{4,5},{5,4},{6,7},{7,6},{8,9},{9,8},{10,11... | collective-permute-start | bytes 786440 | tf_op jit(solution)/shard_map/ppermute | solution.py:8
  30.2 2.4 %collective-permute-start.1 = (bf16[2,256,256]{1,2,0:T(8,128)(2,1)S(1)}, bf16[2,256,256]{1,2,0:T(8,128)(2,1)S(1)}, u32[]{:S(2)}, u32[]{:S(2)}) collective-permute-start(bf16[2,256,256]{1,2,0:T(8,128)(2,1)S(1)} %fusion.28), channel_id=1, source_target_pairs={{0,2},{1,3},{2,0},{3,1},{4,6},{5,7},{6,4},{7,5},{8,10},{9,11},{10,... | collective-permute-start | bytes 786440 | tf_op jit(solution)/shard_map/ppermute | solution.py:8
  33.6 1.4 %pad_maximum_fusion = bf16[2,1536,256]{2,1,0:T(8,128)(2,1)S(1)} fusion(bf16[2,512,256]{2,1,0:T(8,128)(2,1)} %collective-permute-done.4, bf16[2,512,256]{2,1,0:T(8,128)(2,1)S(1)} %convert_element_type.58, bf16[2,512,256]{2,1,0:T(8,128)(2,1)} %collective-permute-done.3), kind=kLoop, calls=%fused_computation | loop fusion | flops 4718592 | bytes 3145728 | tf_op jit(solution)/shard_map/concatenate | solution.py:21
  44.2 14.4 %collective-permute-start.2 = (bf16[2,256,256]{1,2,0:T(8,128)(2,1)S(1)}, bf16[2,256,256]{1,2,0:T(8,128)(2,1)}, u32[]{:S(2)}, u32[]{:S(2)}) collective-permute-start(bf16[2,256,256]{1,2,0:T(8,128)(2,1)S(1)} %fusion.29), channel_id=1, source_target_pairs={{0,4},{1,5},{2,6},{3,7},{4,0},{5,1},{6,2},{7,3},{8,12},{9,13},{10,... | collective-permute-start | bytes 786440 | tf_op jit(solution)/shard_map/ppermute | solution.py:8
  59.6 0.9 fusion.59
  61.6 1.2 %mul.186 = f32[2,4,128,256]{2,1,3,0:T(4,128)} broadcast(f32[2,128,256]{1,2,0:T(8,128)S(1)} %maximum_multiply_fusion), dimensions={0,2,3} | broadcast | bytes 1310720 | tf_op jit(solution)/shard_map/mul | solution.py:67
  62.8 1.6 %mul.187 = f32[2,512,256]{1,2,0:T(8,128)S(1)} reshape(f32[2,4,128,256]{2,1,3,0:T(4,128)} %mul.186) | data formatting | bytes 2097152 | tf_op jit(solution)/shard_map/mul | solution.py:67
  64.6 1.1 %fusion.25 = f32[1,128,256]{1,2,0:T(8,128)S(1)} fusion(f32[256,128]{1,0:T(8,128)} %fusion.118, bf16[2,12,128,256]{3,2,1,0:T(8,128)(2,1)S(1)} %bitcast.424, s32[]{:T(128)S(6)} %select_n.38, bf16[6,2,128,128]{3,2,1,0:T(8,128)(2,1)S(1)} %copy-done.13), kind=kOutput, calls=%fused_computation.52 | convolution fusion | flops 8421376 | bytes 360452 | tf_op jit(solution)/shard_map/dot_general | solution.py:26
  66.3 1.2 %mul.194 = f32[2,4,128,256]{2,1,3,0:T(4,128)} broadcast(f32[2,128,256]{1,2,0:T(8,128)S(1)} %maximum_multiply_fusion.1), dimensions={0,2,3} | broadcast | bytes 1310720 | tf_op jit(solution)/shard_map/mul | solution.py:67
  67.5 2.7 %mul.195 = f32[2,512,256]{1,2,0:T(8,128)} reshape(f32[2,4,128,256]{2,1,3,0:T(4,128)} %mul.194) | data formatting | bytes 2097152 | tf_op jit(solution)/shard_map/mul | solution.py:67
  70.3 1.1 %fusion.23 = f32[1,128,256]{1,2,0:T(8,128)S(1)} fusion(f32[256,128]{1,0:T(8,128)} %fusion.119, bf16[2,12,128,256]{3,2,1,0:T(8,128)(2,1)S(1)} %bitcast.426, s32[]{:T(128)S(6)} %select_n.39, bf16[6,2,128,128]{3,2,1,0:T(8,128)(2,1)S(1)} %copy-done.13), kind=kOutput, calls=%fused_computation.48 | convolution fusion | flops 8421376 | bytes 360452 | tf_op jit(solution)/shard_map/dot_general | solution.py:26
  72.2 1.2 %mul.202 = f32[2,4,128,256]{2,1,3,0:T(4,128)} broadcast(f32[2,128,256]{1,2,0:T(8,128)S(1)} %maximum_multiply_fusion.2), dimensions={0,2,3} | broadcast | bytes 1310720 | tf_op jit(solution)/shard_map/mul | solution.py:67
  73.3 2.6 %mul.203 = f32[2,512,256]{1,2,0:T(8,128)} reshape(f32[2,4,128,256]{2,1,3,0:T(4,128)} %mul.202) | data formatting | bytes 2097152 | tf_op jit(solution)/shard_map/mul | solution.py:67
  76.1 1.1 %fusion.21 = f32[1,128,256]{1,2,0:T(8,128)S(1)} fusion(f32[256,128]{1,0:T(8,128)} %fusion.120, bf16[2,12,128,256]{3,2,1,0:T(8,128)(2,1)S(1)} %bitcast.428, s32[]{:T(128)S(6)} %select_n.40, bf16[6,2,128,128]{3,2,1,0:T(8,128)(2,1)S(1)} %copy-done.13), kind=kOutput, calls=%fused_computation.44 | convolution fusion | flops 8421376 | bytes 360452 | tf_op jit(solution)/shard_map/dot_general | solution.py:26
  77.9 1.2 %mul.210 = f32[2,4,128,256]{2,1,3,0:T(4,128)} broadcast(f32[2,128,256]{1,2,0:T(8,128)S(1)} %maximum_multiply_fusion.3), dimensions={0,2,3} | broadcast | bytes 1310720 | tf_op jit(solution)/shard_map/mul | solution.py:67
  79.1 2.6 %mul.211 = f32[2,512,256]{1,2,0:T(8,128)} reshape(f32[2,4,128,256]{2,1,3,0:T(4,128)} %mul.210) | data formatting | bytes 2097152 | tf_op jit(solution)/shard_map/mul | solution.py:67
  81.9 1.1 %fusion.19 = f32[1,128,256]{1,2,0:T(8,128)S(1)} fusion(f32[256,128]{1,0:T(8,128)} %fusion.121, bf16[2,12,128,256]{3,2,1,0:T(8,128)(2,1)S(1)} %bitcast.430, s32[]{:T(128)S(6)} %select_n.41, bf16[6,2,128,128]{3,2,1,0:T(8,128)(2,1)S(1)} %copy-done.13), kind=kOutput, calls=%fused_computation.40 | convolution fusion | flops 8421376 | bytes 360452 | tf_op jit(solution)/shard_map/dot_general | solution.py:26
  83.7 1.2 %mul.218 = f32[2,4,128,256]{2,1,3,0:T(4,128)} broadcast(f32[2,128,256]{1,2,0:T(8,128)S(1)} %maximum_multiply_fusion.4), dimensions={0,2,3} | broadcast | bytes 1310720 | tf_op jit(solution)/shard_map/mul | solution.py:67
  84.9 2.6 %mul.219 = f32[2,512,256]{1,2,0:T(8,128)} reshape(f32[2,4,128,256]{2,1,3,0:T(4,128)} %mul.218) | data formatting | bytes 2097152 | tf_op jit(solution)/shard_map/mul | solution.py:67
  87.7 1.1 %fusion.17 = f32[1,128,256]{1,2,0:T(8,128)S(1)} fusion(f32[256,128]{1,0:T(8,128)} %fusion.122, bf16[2,12,128,256]{3,2,1,0:T(8,128)(2,1)S(1)} %bitcast.432, s32[]{:T(128)S(6)} %select_n.42, bf16[6,2,128,128]{3,2,1,0:T(8,128)(2,1)S(1)} %copy-done.13), kind=kOutput, calls=%fused_computation.36 | convolution fusion | flops 8421376 | bytes 360452 | tf_op jit(solution)/shard_map/dot_general | solution.py:26
  89.7 1.4 %mul.227 = f32[2,512,256]{1,2,0:T(8,128)} reshape(f32[2,4,128,256]{2,1,3,0:T(4,128)S(1)} %mul.226) | data formatting | bytes 2097152 | tf_op jit(solution)/shard_map/mul | solution.py:67
  91.1 1.2 %fusion.5 = f32[1,256,256]{1,2,0:T(8,128)S(1)} fusion(f32[256,256]{1,0:T(8,128)} %fusion.61, bf16[2,256,256]{1,2,0:T(8,128)(2,1)S(1)} %fusion.29, bf16[3,2,256,256]{3,2,1,0:T(8,128)(2,1)} %param.9), kind=kOutput, calls=%fused_computation.12 | convolution fusion | flops 33619968 | bytes 786432 | tf_op jit(solution)/shard_map/dot_general | solution.py:26
  92.3 1.2 %fusion.4 = f32[1,256,256]{1,2,0:T(8,128)S(1)} fusion(f32[256,256]{1,0:T(8,128)} %fusion.59, bf16[2,256,256]{1,2,0:T(8,128)(2,1)S(1)} %fusion.29, bf16[3,2,256,256]{3,2,1,0:T(8,128)(2,1)} %param.9), kind=kOutput, calls=%fused_computation.10 | convolution fusion | flops 33619968 | bytes 786432 | tf_op jit(solution)/shard_map/dot_general | solution.py:29
  93.6 1.1 %fusion.53 = f32[256,256]{1,0:T(8,128)S(1)} fusion(bf16[2,256,256]{1,2,0:T(8,128)(2,1)} %collective-permute-done.2, bf16[3,2,256,256]{3,2,1,0:T(8,128)(2,1)S(1)} %copy-done.9), kind=kOutput, calls=%fused_computation.107 | convolution fusion | flops 33554432 | bytes 524288 | tf_op jit(solution)/shard_map/dot_general | solution.py:26
  94.7 1.2 %fusion.51 = f32[256,256]{1,0:T(8,128)S(1)} fusion(bf16[2,256,256]{1,2,0:T(8,128)(2,1)} %collective-permute-done.2, bf16[3,2,256,256]{3,2,1,0:T(8,128)(2,1)S(1)} %copy-done.9), kind=kOutput, calls=%fused_computation.105 | convolution fusion | flops 33554432 | bytes 524288 | tf_op jit(solution)/shard_map/dot_general | solution.py:29
  95.9 1.1 %fusion.3 = f32[1,256,256]{1,2,0:T(8,128)S(1)} fusion(f32[256,256]{1,0:T(8,128)S(1)} %fusion.53, bf16[2,256,256]{1,2,0:T(8,128)(2,1)} %collective-permute-done.2, bf16[3,2,256,256]{3,2,1,0:T(8,128)(2,1)S(1)} %copy-done.9), kind=kOutput, calls=%fused_computation.8 | convolution fusion | flops 33619968 | bytes 786432 | tf_op jit(solution)/shard_map/dot_general | solution.py:26
  97.0 1.1 %fusion.2 = f32[1,256,256]{1,2,0:T(8,128)S(1)} fusion(f32[256,256]{1,0:T(8,128)S(1)} %fusion.51, bf16[2,256,256]{1,2,0:T(8,128)(2,1)} %collective-permute-done.2, bf16[3,2,256,256]{3,2,1,0:T(8,128)(2,1)S(1)} %copy-done.9), kind=kOutput, calls=%fused_computation.6 | convolution fusion | flops 33619968 | bytes 786432 | tf_op jit(solution)/shard_map/dot_general | solution.py:29
  100.8 0.9 maximum_add_fusion
  101.8 1.3 %copy.9 = f32[2,512,256]{2,1,0:T(8,128)} copy(f32[2,512,256]{1,2,0:T(8,128)S(1)} %maximum_add_fusion) | data formatting | bytes 2097152 | tf_op jit(solution)/shard_map/add | solution.py:68
  (112 shorter events, 28.2 us)
Async XLA Ops:
  0.0 10.7 %copy-start = (s32[512,6,3]{0,2,1:T(4,128)S(1)}, s32[512,6,3]{0,2,1:T(4,128)}, u32[]{:S(2)}) copy-start(s32[512,6,3]{0,2,1:T(4,128)} %param.13) | copy-start | bytes 110596
  0.0 7.0 %copy-start.10 = (bf16[2,256,512]{2,1,0:T(8,128)(2,1)S(1)}, bf16[2,256,512]{2,1,0:T(8,128)(2,1)}, u32[]{:S(2)}) copy-start(bf16[2,256,512]{2,1,0:T(8,128)(2,1)} %param.8) | copy-start | bytes 1572868
  1.3 32.2 %collective-permute-start.3 = (bf16[2,512,256]{2,1,0:T(8,128)(2,1)S(1)}, bf16[2,512,256]{2,1,0:T(8,128)(2,1)}, u32[]{:S(2)}, u32[]{:S(2)}) collective-permute-start(bf16[2,512,256]{2,1,0:T(8,128)(2,1)S(1)} %convert_element_type.58), channel_id=1, source_target_pairs={{0,1},{1,2},{2,3},{3,4},{4,5},{5,6},{6,7},{7,8},{8,9},{9,10},{10,1... | collective-permute-start | bytes 1572872 | tf_op jit(solution)/shard_map/ppermute | solution.py:17
  5.1 28.4 %collective-permute-start.4 = (bf16[2,512,256]{2,1,0:T(8,128)(2,1)S(1)}, bf16[2,512,256]{2,1,0:T(8,128)(2,1)}, u32[]{:S(2)}, u32[]{:S(2)}) collective-permute-start(bf16[2,512,256]{2,1,0:T(8,128)(2,1)S(1)} %convert_element_type.58), channel_id=1, source_target_pairs={{1,0},{2,1},{3,2},{4,3},{5,4},{6,5},{7,6},{8,7},{9,8},{10,9},{11,1... | collective-permute-start | bytes 1572872 | tf_op jit(solution)/shard_map/ppermute | solution.py:20
  7.3 3.6 %copy-start.6 = (bf16[3,2,256,256]{3,2,1,0:T(8,128)(2,1)S(1)}, bf16[3,2,256,256]{3,2,1,0:T(8,128)(2,1)}, u32[]{:S(2)}) copy-start(bf16[3,2,256,256]{3,2,1,0:T(8,128)(2,1)} %param.9) | copy-start | bytes 2359300
  8.0 21.2 %copy-start.7 = (bf16[3,2,256,256]{3,2,1,0:T(8,128)(2,1)S(1)}, bf16[3,2,256,256]{3,2,1,0:T(8,128)(2,1)}, u32[]{:S(2)}) copy-start(bf16[3,2,256,256]{3,2,1,0:T(8,128)(2,1)} %param.10) | copy-start | bytes 2359300
  8.1 21.2 %collective-permute-start = (bf16[2,256,256]{2,1,0:T(8,128)(2,1)S(1)}, bf16[2,256,256]{2,1,0:T(8,128)(2,1)S(1)}, u32[]{:S(2)}, u32[]{:S(2)}) collective-permute-start(bf16[2,256,256]{2,1,0:T(8,128)(2,1)S(1)} %pad_maximum_fusion.1), channel_id=1, source_target_pairs={{0,1},{1,0},{2,3},{3,2},{4,5},{5,4},{6,7},{7,6},{8,9},{9,8},{10,11... | collective-permute-start | bytes 786440 | tf_op jit(solution)/shard_map/ppermute | solution.py:8
  30.2 13.0 %collective-permute-start.1 = (bf16[2,256,256]{1,2,0:T(8,128)(2,1)S(1)}, bf16[2,256,256]{1,2,0:T(8,128)(2,1)S(1)}, u32[]{:S(2)}, u32[]{:S(2)}) collective-permute-start(bf16[2,256,256]{1,2,0:T(8,128)(2,1)S(1)} %fusion.28), channel_id=1, source_target_pairs={{0,2},{1,3},{2,0},{3,1},{4,6},{5,7},{6,4},{7,5},{8,10},{9,11},{10,... | collective-permute-start | bytes 786440 | tf_op jit(solution)/shard_map/ppermute | solution.py:8
  33.5 1.4 %copy-start.12 = (bf16[6,2,128,128]{3,2,1,0:T(8,128)(2,1)S(1)}, bf16[6,2,128,128]{3,2,1,0:T(8,128)(2,1)}, u32[]{:S(2)}) copy-start(bf16[6,2,128,128]{3,2,1,0:T(8,128)(2,1)} %param.12) | copy-start | bytes 1179652
  34.9 8.3 %copy-start.8 = (bf16[3,2,256,256]{3,2,1,0:T(8,128)(2,1)S(1)}, bf16[3,2,256,256]{3,2,1,0:T(8,128)(2,1)}, u32[]{:S(2)}) copy-start(bf16[3,2,256,256]{3,2,1,0:T(8,128)(2,1)} %param.10) | copy-start | bytes 2359300
  44.2 49.4 %collective-permute-start.2 = (bf16[2,256,256]{1,2,0:T(8,128)(2,1)S(1)}, bf16[2,256,256]{1,2,0:T(8,128)(2,1)}, u32[]{:S(2)}, u32[]{:S(2)}) collective-permute-start(bf16[2,256,256]{1,2,0:T(8,128)(2,1)S(1)} %fusion.29), channel_id=1, source_target_pairs={{0,4},{1,5},{2,6},{3,7},{4,0},{5,1},{6,2},{7,3},{8,12},{9,13},{10,... | collective-permute-start | bytes 786440 | tf_op jit(solution)/shard_map/ppermute | solution.py:8
  61.6 2.8 %copy-start.13 = (bf16[6,2,128,128]{3,2,1,0:T(8,128)(2,1)S(1)}, bf16[6,2,128,128]{3,2,1,0:T(8,128)(2,1)}, u32[]{:S(2)}) copy-start(bf16[6,2,128,128]{3,2,1,0:T(8,128)(2,1)} %param.12) | copy-start | bytes 1179652
  66.3 3.8 %copy-start.17 = (f32[256,128]{1,0:T(8,128)S(1)}, f32[256,128]{1,0:T(8,128)}, u32[]{:S(2)}) copy-start(f32[256,128]{1,0:T(8,128)} %fusion.113) | copy-start | bytes 393220
  72.2 3.8 %copy-start.16 = (f32[256,128]{1,0:T(8,128)S(1)}, f32[256,128]{1,0:T(8,128)}, u32[]{:S(2)}) copy-start(f32[256,128]{1,0:T(8,128)} %fusion.114) | copy-start | bytes 393220
  77.9 3.8 %copy-start.15 = (f32[256,128]{1,0:T(8,128)S(1)}, f32[256,128]{1,0:T(8,128)}, u32[]{:S(2)}) copy-start(f32[256,128]{1,0:T(8,128)} %fusion.115) | copy-start | bytes 393220
  83.7 3.8 %copy-start.14 = (f32[256,128]{1,0:T(8,128)S(1)}, f32[256,128]{1,0:T(8,128)}, u32[]{:S(2)}) copy-start(f32[256,128]{1,0:T(8,128)} %fusion.116) | copy-start | bytes 393220
  89.7 3.9 %copy-start.9 = (bf16[3,2,256,256]{3,2,1,0:T(8,128)(2,1)S(1)}, bf16[3,2,256,256]{3,2,1,0:T(8,128)(2,1)}, u32[]{:S(2)}) copy-start(bf16[3,2,256,256]{3,2,1,0:T(8,128)(2,1)} %param.10) | copy-start | bytes 2359300
  94.7 3.6 %copy-start.11 = (bf16[2,512,256]{2,1,0:T(8,128)(2,1)S(1)}, bf16[2,512,256]{2,1,0:T(8,128)(2,1)}, u32[]{:S(2)}) copy-start(bf16[2,512,256]{2,1,0:T(8,128)(2,1)} %param.11) | copy-start | bytes 1572868
  98.2 1.2 %copy-start.5 = (f32[2,512,256]{1,2,0:T(8,128)S(1)}, f32[2,512,256]{1,2,0:T(8,128)}, u32[]{:S(2)}) copy-start(f32[2,512,256]{1,2,0:T(8,128)} %mul.227) | copy-start | bytes 3145732
  98.3 1.5 %copy-start.4 = (f32[2,512,256]{1,2,0:T(8,128)S(1)}, f32[2,512,256]{1,2,0:T(8,128)}, u32[]{:S(2)}) copy-start(f32[2,512,256]{1,2,0:T(8,128)} %mul.219) | copy-start | bytes 3145732
  98.6 1.6 %copy-start.3 = (f32[2,512,256]{1,2,0:T(8,128)S(1)}, f32[2,512,256]{1,2,0:T(8,128)}, u32[]{:S(2)}) copy-start(f32[2,512,256]{1,2,0:T(8,128)} %mul.211) | copy-start | bytes 3145732
  98.8 1.7 %copy-start.1 = (f32[2,512,256]{1,2,0:T(8,128)S(1)}, f32[2,512,256]{1,2,0:T(8,128)}, u32[]{:S(2)}) copy-start(f32[2,512,256]{1,2,0:T(8,128)} %mul.195) | copy-start | bytes 3145732
  98.8 2.0 %copy-start.2 = (f32[2,512,256]{1,2,0:T(8,128)S(1)}, f32[2,512,256]{1,2,0:T(8,128)}, u32[]{:S(2)}) copy-start(f32[2,512,256]{1,2,0:T(8,128)} %mul.203) | copy-start | bytes 3145732
where the time goes:
time: 104 us; the launch traced here: 103 us
  matrix products  29.5 us (28%)
  starting transfers between devices  25.1 us (24%)
  local copies, waits for them, and re-layouts  24.7 us (24%)
  between operations  12.1 us (12%)
  other arithmetic  11.6 us (11%)
    mul x15, local copies, waits for them, and re-layouts, per_device(): near = near + term[:, None] * hit[None, :, None, None]  19.7 us
    ppermute x3, starting transfers between devices, from_partner(): lax.ppermute(x, axis, [(i, i ^ 1 << apart) for i in range(lax.axis_size(a...  19.4 us
    dot_general x14, matrix products, cmat(): jnp.dot(matrix[0], vector[0], preferred_element_type=jnp.float32)  9.13 us
    dot_general x14, matrix products, cmat(): jnp.dot(matrix[1], vector[1], preferred_element_type=jnp.float32)  8.22 us
    dot_general x14, matrix products, cmat(): jnp.dot(matrix[1], vector[0], preferred_element_type=jnp.float32)  7.55 us
    dot_general x14, matrix products, cmat(): jnp.dot(matrix[0], vector[1], preferred_element_type=jnp.float32)  4.62 us
    mul x6, other arithmetic, per_device(): term = cmat(near_tiles[slot], block) * valid[slot]  4.12 us
    ppermute x1, starting transfers between devices, extended(): lax.ppermute(lax.slice_in_dim(block, block.shape[dim] - width, None, axis...  3.77 us
  transfers between devices with their start and end apart: 5, of which 0 were waited for; matrix products, arithmetic and copies ran while one was open for 53% of the time, Pallas kernels for 0%

commit v1 on v0

v1 whole, which is shorter than its diff:
```python
import functools

import jax
import jax.numpy as jnp
from jax import lax
from jax.experimental import pallas as pl
from jax.experimental.pallas import tpu as pltpu
from jax.sharding import PartitionSpec as P

MESH = pl.DeviceIdType.MESH
CHUNKS = 2


def cmul(real, imag, block):
    half = block.shape[-1] // 2
    turned = jnp.concatenate([-block[:, half:], block[:, :half]], axis=1)
    return jnp.dot(real, block, preferred_element_type=jnp.float32) + jnp.dot(
        imag, turned, preferred_element_type=jnp.float32
    )


def kernel(
    n,
    x_hbm,
    leaf_hbm,
    self_hbm,
    cross_hbm,
    out_hbm,
    tiles_hbm,
    list_hbm,
    o_hbm,
    xf,
    xb,
    window,
    leaf,
    own,
    cross,
    outb,
    tiles,
    listed,
    near_send,
    near_recv,
    coef,
    got,
    terms,
    near,
    ostage,
    load_sem,
    near_ssem,
    near_rsem,
    send_sem,
    recv_sem,
    store_sem,
):
    me = lax.axis_index("surf")
    left = lax.rem(me + n - 1, n)
    right = lax.rem(me + 1, n)
    levels = own.shape[0]
    blocks, tile, wide = xb.shape
    width = wide // 2
    part = width // CHUNKS
    slots = tiles.shape[0]

    barrier = pltpu.get_barrier_semaphore()
    peers = [left, right] + [me ^ (1 << l) for l in range(levels)]
    for peer in peers:
        pl.semaphore_signal(barrier, inc=1, device_id=(peer,), device_id_type=MESH)

    loads = {}

    def load(name, src, dst):
        loads[name] = pltpu.make_async_copy(src, dst, load_sem.at[len(loads)])
        loads[name].start()

    load("x", x_hbm, xf)
    load("leaf", leaf_hbm, leaf)
    load("list", list_hbm, listed)
    for l in range(levels):
        load(f"self{l}", self_hbm.at[l], own.at[l])
        load(f"cross{l}", cross_hbm.at[l], cross.at[l])
    load("tiles", tiles_hbm, tiles)
    load("out", out_hbm, outb)

    loads["x"].wait()
    for b in range(blocks):
        rows = slice(b * tile, (b + 1) * tile)
        both = jnp.concatenate([xf[0, rows, :], xf[1, rows, :]], axis=1).astype(jnp.bfloat16)
        xb[b] = both
        window[b] = both

    def chunk(c):
        lo, hi = c * part, (c + 1) * part
        rows = blocks * tile
        real = xb[:, :, lo:hi].reshape(rows, part)
        imag = xb[:, :, width + lo : width + hi].reshape(rows, part)
        return jnp.concatenate([real, imag], axis=1)

    def exchange(level, c):
        return pltpu.make_async_remote_copy(
            src_ref=coef.at[level, c],
            dst_ref=got.at[level, c],
            send_sem=send_sem.at[level, c],
            recv_sem=recv_sem.at[level, c],
            device_id=(me ^ (1 << level),),
            device_id_type=MESH,
        )

    loads["list"].wait()

    def listed_span(patch, owner):
        low, high = jnp.int32(blocks), jnp.int32(-1)
        for k in range(slots):
            hit = listed[k, 0, patch] == owner
            col = listed[k, 2, patch]
            low = jnp.minimum(low, jnp.where(hit, col, blocks))
            high = jnp.maximum(high, jnp.where(hit, col, -1))
        return jnp.where(high < 0, 0, low), jnp.maximum(high, 0)

    pl.semaphore_wait(barrier, len(peers))
    near_copies = []
    for s, (patch, landing) in enumerate(((left, 1), (right, 0))):
        low, high = listed_span(patch, me)
        near_send[s, 0] = xb[low]
        near_send[s, 1] = xb[high]
        copy = pltpu.make_async_remote_copy(
            src_ref=near_send.at[s],
            dst_ref=near_recv.at[landing],
            send_sem=near_ssem.at[s],
            recv_sem=near_rsem.at[landing],
            device_id=(patch,),
            device_id_type=MESH,
        )
        copy.start()
        near_copies.append(copy)

    loads["leaf"].wait()
    copies = {}
    for c in range(CHUNKS):
        coef[0, c] = cmul(leaf[0], leaf[1], chunk(c)).astype(jnp.bfloat16)
        copies[0, c] = exchange(0, c)
        copies[0, c].start()

    def near_field():
        loads["tiles"].wait()
        for copy in near_copies:
            copy.wait_recv()
        for s in range(2):
            for h in range(2):
                window[blocks + 2 * s + h] = near_recv[s, h]
        low_left, _ = listed_span(me, left)
        low_right, _ = listed_span(me, right)
        hits = []
        for k in range(slots):
            owner, row, col = listed[k, 0, me], listed[k, 1, me], listed[k, 2, me]
            place = jnp.where(
                owner == left,
                blocks + (col != low_left).astype(jnp.int32),
                jnp.where(owner == right, blocks + 2 + (col != low_right).astype(jnp.int32), col),
            )
            hits.append(jnp.where(owner >= 0, row, -1))
            terms[k] = cmul(tiles[k, 0], tiles[k, 1], window[place])
        for r in range(blocks):
            total = jnp.zeros((tile, wide), jnp.float32)
            for k in range(slots):
                total = total + terms[k] * jnp.where(hits[k] == r, 1.0, 0.0)
            near[r * tile : (r + 1) * tile, :] = total

    stores = []
    for l in range(levels):
        loads[f"self{l}"].wait()
        sums = [cmul(own[l, 0], own[l, 1], coef[l, c]) for c in range(CHUNKS)]
        if l == 1:
            near_field()
        loads[f"cross{l}"].wait()
        for c in range(CHUNKS):
            copies[l, c].wait_recv()
            after = (sums[c] + cmul(cross[l, 0], cross[l, 1], got[l, c])).astype(jnp.bfloat16)
            if l + 1 < levels:
                coef[l + 1, c] = after
                copies[l + 1, c] = exchange(l + 1, c)
                copies[l + 1, c].start()
                continue
            if c == 0:
                loads["out"].wait()
            far = cmul(outb[0], outb[1], after)
            lo, hi = c * part, (c + 1) * part
            ostage[0, :, lo:hi] = far[:, :part] + near[:, lo:hi]
            ostage[1, :, lo:hi] = far[:, part:] + near[:, width + lo : width + hi]
            store = pltpu.make_async_copy(
                ostage.at[:, :, lo:hi], o_hbm.at[:, :, lo:hi], store_sem.at[c]
            )
            store.start()
            stores.append(store)
    for copy in near_copies:
        copy.wait_send()
    for copy in copies.values():
        copy.wait_send()
    for store in stores:
        store.wait()


def per_device(
    excitation, leaf_basis, self_transfer, cross_transfer, out_basis, near_tiles, near_list
):
    n = lax.axis_size("surf")
    rows, width = excitation.shape[1:]
    rank = leaf_basis.shape[1]
    levels = self_transfer.shape[0]
    slots, _, tile, _ = near_tiles.shape
    blocks = rows // tile
    by_slot = jnp.transpose(near_list, (1, 2, 0))
    half, full = jnp.bfloat16, jnp.float32
    anywhere = pl.BlockSpec(memory_space=pl.ANY)
    part = 2 * width // CHUNKS
    return pl.pallas_call(
        functools.partial(kernel, n),
        out_shape=jax.ShapeDtypeStruct(excitation.shape, full),
        in_specs=[anywhere] * 7,
        out_specs=anywhere,
        scratch_shapes=[
            pltpu.VMEM(excitation.shape, full),
            pltpu.VMEM((blocks, tile, 2 * width), half),
            pltpu.VMEM((blocks + 4, tile, 2 * width), half),
            pltpu.VMEM(leaf_basis.shape, half),
            pltpu.VMEM(self_transfer.shape, half),
            pltpu.VMEM(cross_transfer.shape, half),
            pltpu.VMEM(out_basis.shape, half),
            pltpu.VMEM(near_tiles.shape, half),
            pltpu.SMEM(by_slot.shape, jnp.int32),
            pltpu.VMEM((2, 2, tile, 2 * width), half),
            pltpu.VMEM((2, 2, tile, 2 * width), half),
            pltpu.VMEM((levels, CHUNKS, rank, part), half),
            pltpu.VMEM((levels, CHUNKS, rank, part), half),
            pltpu.VMEM((slots, tile, 2 * width), full),
            pltpu.VMEM((rows, 2 * width), full),
            pltpu.VMEM(excitation.shape, full),
            pltpu.SemaphoreType.DMA((5 + 2 * levels,)),
            pltpu.SemaphoreType.DMA((2,)),
            pltpu.SemaphoreType.DMA((2,)),
            pltpu.SemaphoreType.DMA((levels, CHUNKS)),
            pltpu.SemaphoreType.DMA((levels, CHUNKS)),
            pltpu.SemaphoreType.DMA((CHUNKS,)),
        ],
        compiler_params=pltpu.CompilerParams(collective_id=0, has_side_effects=True),
    )(
        excitation,
        leaf_basis,
        self_transfer,
        cross_transfer,
        out_basis,
        near_tiles,
        by_slot,
    )


def solution(mesh):
    placed = (
        P(None, "surf", None),
        P(None, "surf", None),
        P(None, None, "surf", None),
        P(None, None, "surf", None),
        P(None, "surf", None),
        P("surf", None, None, None),
        P(),
    )
    return jax.shard_map(
        per_device, mesh=mesh, in_specs=placed, out_specs=P(None, "surf", None), check_vma=False
    )
```

time: 104 us -> 33 us (0.32)
  the two profiles are of different devices: /device:TPU:25 before, /device:TPU:16 now
where the time goes in v1:
time: 33 us; the launch traced here: 32.8 us
  Pallas kernels  30.6 us (93%)
  local copies, waits for them, and re-layouts  2.26 us (7%)
    pallas_call x1, Pallas kernels, per_device(): pl.pallas_call(functools.partial(kernel, n), out_shape=jax.ShapeDtypeStru...  30.6 us
    unnamed x1, local copies, waits for them, and re-layouts  2.26 us

profile of v1, /device:TPU:16, one launch (start us, length us, event | category | flops | bytes accessed | tf_op | source)
XLA Modules:
  0.0 32.8 jit_solution(9952708429275051625)
XLA Ops:
  0.0 30.6 %shard_map.73 = f32[2,512,256]{2,1,0:T(8,128)} custom-call(f32[2,512,256]{2,1,0:T(8,128)} %x_hbm.1, bf16[2,256,512]{2,1,0:T(8,128)(2,1)} %leaf_hbm.1, bf16[3,2,256,256]{3,2,1,0:T(8,128)(2,1)} %self_hbm.1, bf16[3,2,256,256]{3,2,1,0:T(8,128)(2,1)} %cross_hbm.1, bf16[2,512,256]{2,1,0:T(8,128)(2,1)} %out_hbm.1, bf16[6,2,128,128]{3,2,1,0:T(8,128)(2,1)} %tiles_hbm.1, ...), custom_call_target="tpu_custom_call" | custom-call | tf_op jit(solution)/shard_map/pallas_call | solution.py:215
  30.6 2.3 %copy.9 = f32[2,512,256]{2,1,0:T(8,128)} copy(f32[2,512,256]{2,1,0:T(8,128)} %shard_map.73) | data formatting | bytes 2097152

commit v2 on v1

--- a/solution.py
+++ b/solution.py
@@ -13,10 +13,13 @@
 
 def cmul(real, imag, block):
     half = block.shape[-1] // 2
-    turned = jnp.concatenate([-block[:, half:], block[:, :half]], axis=1)
-    return jnp.dot(real, block, preferred_element_type=jnp.float32) + jnp.dot(
-        imag, turned, preferred_element_type=jnp.float32
-    )
+    plain = jnp.dot(real, block, preferred_element_type=jnp.float32)
+    if half % 128 == 0:
+        turned = jnp.concatenate([-block[:, half:], block[:, :half]], axis=1)
+        return plain + jnp.dot(imag, turned, preferred_element_type=jnp.float32)
+    other = pltpu.roll(jnp.dot(imag, block, preferred_element_type=jnp.float32), half, 1)
+    lane = lax.broadcasted_iota(jnp.int32, other.shape, 1)
+    return plain + jnp.where(lane < half, -other, other)
 
 
 def kernel(
@@ -28,7 +31,7 @@
     out_hbm,
     tiles_hbm,
     list_hbm,
-    o_hbm,
+    o_ref,
     xf,
     xb,
     window,
@@ -44,27 +47,49 @@
     got,
     terms,
     near,
-    ostage,
     load_sem,
     near_ssem,
     near_rsem,
     send_sem,
     recv_sem,
-    store_sem,
+    ready,
 ):
     me = lax.axis_index("surf")
-    left = lax.rem(me + n - 1, n)
-    right = lax.rem(me + 1, n)
     levels = own.shape[0]
     blocks, tile, wide = xb.shape
     width = wide // 2
     part = width // CHUNKS
     slots = tiles.shape[0]
-
+    group = 1 << levels
+
+    def parity(device):
+        return lax.rem(sum(lax.rem(device // (1 << l), 2) for l in range(levels)), 2)
+
+    odd = lax.rem(me, 2)
+    left = lax.rem(me + n - 1, n)
+    right = lax.rem(me + 1, n)
+    mate = me ^ 1
+    beside = lax.rem(me + n - 1 + 2 * odd, n)
+    place = lax.rem(me, group)
+    last_side = levels
+    hub = parity(me) == 0
+    answers_beside = jnp.where(parity(me) != parity(beside), parity(me) == 0, odd == 1)
     barrier = pltpu.get_barrier_semaphore()
-    peers = [left, right] + [me ^ (1 << l) for l in range(levels)]
-    for peer in peers:
-        pl.semaphore_signal(barrier, inc=1, device_id=(peer,), device_id_type=MESH)
+
+    def greet(device):
+        pl.semaphore_signal(barrier, inc=1, device_id=(device,), device_id_type=MESH)
+
+    def answer(device, which):
+        pl.semaphore_signal(ready.at[which], inc=1, device_id=(device,), device_id_type=MESH)
+
+    @pl.when(jnp.logical_not(hub))
+    def _():
+        for l in range(levels):
+            greet(me ^ (1 << l))
+
+    @pl.when(jnp.logical_not(answers_beside))
+    def _():
+        greet(beside)
 
     loads = {}
 
@@ -80,6 +105,32 @@
         load(f"cross{l}", cross_hbm.at[l], cross.at[l])
     load("tiles", tiles_hbm, tiles)
     load("out", out_hbm, outb)
+
+    @pl.when(jnp.logical_and(hub, answers_beside))
+    def _():
+        pl.semaphore_wait(barrier, levels + 1)
+
+    @pl.when(jnp.logical_and(hub, jnp.logical_not(answers_beside)))
+    def _():
+        pl.semaphore_wait(barrier, levels)
+
+    @pl.when(jnp.logical_and(jnp.logical_not(hub), answers_beside))
+    def _():
+        pl.semaphore_wait(barrier, 1)
+
+    @pl.when(hub)
+    def _():
+        for l in range(levels):
+            answer(me ^ (1 << l), l)
+
+    @pl.when(answers_beside)
+    def _():
+        answer(beside, last_side)
+
+    def until_ready(level):
+        @pl.when(jnp.logical_not(hub))
+        def _():
+            pl.semaphore_wait(ready.at[level], 1)
 
     loads["x"].wait()
     for b in range(blocks):
@@ -105,8 +156,6 @@
             device_id_type=MESH,
         )
 
-    loads["list"].wait()
-
     def listed_span(patch, owner):
         low, high = jnp.int32(blocks), jnp.int32(-1)
         for k in range(slots):
@@ -116,29 +165,46 @@
             high = jnp.maximum(high, jnp.where(hit, col, -1))
         return jnp.where(high < 0, 0, low), jnp.maximum(high, 0)
 
-    pl.semaphore_wait(barrier, len(peers))
-    near_copies = []
-    for s, (patch, landing) in enumerate(((left, 1), (right, 0))):
-        low, high = listed_span(patch, me)
-        near_send[s, 0] = xb[low]
-        near_send[s, 1] = xb[high]
-        copy = pltpu.make_async_remote_copy(
-            src_ref=near_send.at[s],
-            dst_ref=near_recv.at[landing],
-            send_sem=near_ssem.at[s],
-            recv_sem=near_rsem.at[landing],
-            device_id=(patch,),
+    def near_copy(side, device):
+        return pltpu.make_async_remote_copy(
+            src_ref=near_send.at[side],
+            dst_ref=near_recv.at[side],
+            send_sem=near_ssem.at[side],
+            recv_sem=near_rsem.at[side],
+            device_id=(device,),
             device_id_type=MESH,
         )
-        copy.start()
-        near_copies.append(copy)
+
+    near_copies = [near_copy(0, mate), near_copy(1, beside)]
+
+    def send_near(side, device):
+        low, high = listed_span(device, me)
+        near_send[side, 0] = xb[low]
+        near_send[side, 1] = xb[high]
+        near_copies[side].start()
+
+    def send_beside(when):
+        @pl.when(when)
+        def _():
+            @pl.when(jnp.logical_not(answers_beside))
+            def _():
+                pl.semaphore_wait(ready.at[last_side], 1)
+
+            send_near(1, beside)
+
+    first, last = place == 0, place == group - 1
+    loads["list"].wait()
+    send_beside(jnp.logical_not(jnp.logical_or(first, last)))
 
     loads["leaf"].wait()
     copies = {}
     for c in range(CHUNKS):
         coef[0, c] = cmul(leaf[0], leaf[1], chunk(c)).astype(jnp.bfloat16)
         copies[0, c] = exchange(0, c)
+        if c == 0:
+            until_ready(0)
         copies[0, c].start()
+    send_near(0, mate)
 
     def near_field():
         loads["tiles"].wait()
@@ -147,29 +213,31 @@
         for s in range(2):
             for h in range(2):
                 window[blocks + 2 * s + h] = near_recv[s, h]
-        low_left, _ = listed_span(me, left)
-        low_right, _ = listed_span(me, right)
+        low_mate, _ = listed_span(me, mate)
+        low_beside, _ = listed_span(me, beside)
         hits = []
         for k in range(slots):
             owner, row, col = listed[k, 0, me], listed[k, 1, me], listed[k, 2, me]
-            place = jnp.where(
-                owner == left,
-                blocks + (col != low_left).astype(jnp.int32),
-                jnp.where(owner == right, blocks + 2 + (col != low_right).astype(jnp.int32), col),
+            at = jnp.where(
+                owner == mate,
+                blocks + (col != low_mate).astype(jnp.int32),
+                jnp.where(owner == beside, blocks + 2 + (col != low_beside).astype(jnp.int32), col),
             )
             hits.append(jnp.where(owner >= 0, row, -1))
-            terms[k] = cmul(tiles[k, 0], tiles[k, 1], window[place])
+            terms[k] = cmul(tiles[k, 0], tiles[k, 1], window[at])
         for r in range(blocks):
             total = jnp.zeros((tile, wide), jnp.float32)
             for k in range(slots):
                 total = total + terms[k] * jnp.where(hits[k] == r, 1.0, 0.0)
             near[r * tile : (r + 1) * tile, :] = total
 
-    stores = []
     for l in range(levels):
         loads[f"self{l}"].wait()
         sums = [cmul(own[l, 0], own[l, 1], coef[l, c]) for c in range(CHUNKS)]
         if l == 1:
+            send_beside(first)
+        if l + 1 == levels:
+            send_beside(last)
             near_field()
         loads[f"cross{l}"].wait()
         for c in range(CHUNKS):
@@ -178,25 +246,20 @@
             if l + 1 < levels:
                 coef[l + 1, c] = after
                 copies[l + 1, c] = exchange(l + 1, c)
+                if c == 0:
+                    until_ready(l + 1)
                 copies[l + 1, c].start()
                 continue
             if c == 0:
                 loads["out"].wait()
             far = cmul(outb[0], outb[1], after)
             lo, hi = c * part, (c + 1) * part
-            ostage[0, :, lo:hi] = far[:, :part] + near[:, lo:hi]
-            ostage[1, :, lo:hi] = far[:, part:] + near[:, width + lo : width + hi]
-            store = pltpu.make_async_copy(
-                ostage.at[:, :, lo:hi], o_hbm.at[:, :, lo:hi], store_sem.at[c]
-            )
-            store.start()
-            stores.append(store)
+            o_ref[0, :, lo:hi] = far[:, :part] + near[:, lo:hi]
+            o_ref[1, :, lo:hi] = far[:, part:] + near[:, width + lo : width + hi]
     for copy in near_copies:
         copy.wait_send()
     for copy in copies.values():
         copy.wait_send()
-    for store in stores:
-        store.wait()
 
 
 def per_device(
@@ -214,9 +277,9 @@
     part = 2 * width // CHUNKS
     return pl.pallas_call(
         functools.partial(kernel, n),
-        out_shape=jax.ShapeDtypeStruct(excitation.shape, full),
+        out_shape=pltpu.VMEM(excitation.shape, full),
         in_specs=[anywhere] * 7,
-        out_specs=anywhere,
+        out_specs=pl.BlockSpec(memory_space=pltpu.VMEM),
         scratch_shapes=[
             pltpu.VMEM(excitation.shape, full),
             pltpu.VMEM((blocks, tile, 2 * width), half),
@@ -233,23 +296,29 @@
             pltpu.VMEM((levels, CHUNKS, rank, part), half),
             pltpu.VMEM((slots, tile, 2 * width), full),
             pltpu.VMEM((rows, 2 * width), full),
-            pltpu.VMEM(excitation.shape, full),
             pltpu.SemaphoreType.DMA((5 + 2 * levels,)),
             pltpu.SemaphoreType.DMA((2,)),
             pltpu.SemaphoreType.DMA((2,)),
             pltpu.SemaphoreType.DMA((levels, CHUNKS)),
             pltpu.SemaphoreType.DMA((levels, CHUNKS)),
-            pltpu.SemaphoreType.DMA((CHUNKS,)),
+            pltpu.SemaphoreType.REGULAR((levels + 1,)),
         ],
-        compiler_params=pltpu.CompilerParams(collective_id=0, has_side_effects=True),
+        compiler_params=pltpu.CompilerParams(
+            collective_id=0, has_side_effects=True, vmem_limit_bytes=24 << 20
+        ),
     )(
-        excitation,
-        leaf_basis,
-        self_transfer,
-        cross_transfer,
-        out_basis,
-        near_tiles,
-        by_slot,
+        *(
+            pltpu.with_memory_space_constraint(array, pltpu.HBM)
+            for array in (
+                excitation,
+                leaf_basis,
+                self_transfer,
+                cross_transfer,
+                out_basis,
+                near_tiles,
+                by_slot,
+            )
+        )
     )
 
 

time: 33 us -> 32 us (0.970)
  the two profiles are of different devices: /device:TPU:16 before, /device:TPU:6 now
where the time goes in v2:
time: 32 us; the launch traced here: 31.9 us
  Pallas kernels  30.9 us (97%)
  local copies, waits for them, and re-layouts  0.97 us (3%)
    pallas_call x1, Pallas kernels, per_device(): pl.pallas_call(functools.partial(kernel, n), out_shape=pltpu.VMEM(excitat...  30.9 us
    unnamed x1, local copies, waits for them, and re-layouts  0.97 us

profile of v2, /device:TPU:6, one launch (start us, length us, event | category | flops | bytes accessed | tf_op | source)
XLA Modules:
  0.0 31.9 jit_solution(14444971054578339571)
XLA Ops:
  0.0 30.9 %shard_map.73 = f32[2,512,256]{2,1,0:T(8,128)S(1)} custom-call(f32[2,512,256]{2,1,0:T(8,128)} %x_hbm.1, bf16[2,256,512]{2,1,0:T(8,128)(2,1)} %leaf_hbm.1, bf16[3,2,256,256]{3,2,1,0:T(8,128)(2,1)} %self_hbm.1, bf16[3,2,256,256]{3,2,1,0:T(8,128)(2,1)} %cross_hbm.1, bf16[2,512,256]{2,1,0:T(8,128)(2,1)} %out_hbm.1, bf16[6,2,128,128]{3,2,1,0:T(8,128)(2,1)} %tiles_hbm.1, ...), custom_call_target="tpu_custom_call" | custom-call | tf_op jit(solution)/shard_map/pallas_call | solution.py:278
  30.9 1.0 %copy.9 = f32[2,512,256]{2,1,0:T(8,128)} copy(f32[2,512,256]{2,1,0:T(8,128)S(1)} %shard_map.73) | data formatting | bytes 2097152

commit v3 on v2

--- a/solution.py
+++ b/solution.py
@@ -9,6 +9,7 @@
 
 MESH = pl.DeviceIdType.MESH
 CHUNKS = 2
+SHEET = 128
 
 
 def cmul(real, imag, block):
@@ -73,7 +74,7 @@
     place = lax.rem(me, group)
     last_side = levels
     hub = parity(me) == 0
-    answers_beside = jnp.where(parity(me) != parity(beside), parity(me) == 0, odd == 1)
+    answers_beside = odd == 1
     barrier = pltpu.get_barrier_semaphore()
 
     def greet(device):
@@ -192,9 +193,10 @@
 
             send_near(1, beside)
 
-    first, last = place == 0, place == group - 1
+    first = place == 0
+    edge = lax.rem(me, SHEET) == 0
     loads["list"].wait()
-    send_beside(jnp.logical_not(jnp.logical_or(first, last)))
+    send_beside(jnp.logical_not(first))
 
     loads["leaf"].wait()
     copies = {}
@@ -205,6 +207,7 @@
             until_ready(0)
         copies[0, c].start()
     send_near(0, mate)
+    send_beside(jnp.logical_and(first, jnp.logical_not(edge)))
 
     def near_field():
         loads["tiles"].wait()
@@ -234,10 +237,8 @@
     for l in range(levels):
         loads[f"self{l}"].wait()
         sums = [cmul(own[l, 0], own[l, 1], coef[l, c]) for c in range(CHUNKS)]
-        if l == 1:
-            send_beside(first)
         if l + 1 == levels:
-            send_beside(last)
+            send_beside(edge)
             near_field()
         loads[f"cross{l}"].wait()
         for c in range(CHUNKS):

time: 32 us -> 25.2 us (0.79)
  Pallas kernels: 30.9 us -> 24.1 us
    pallas_call x1, Pallas kernels: 30.9 us -> 24.1 us  [per_device(): pl.pallas_call(functools.partial(kernel, n), out_shape=pltpu.VMEM(excitat...]
where the time goes in v3:
time: 25.2 us; the launch traced here: 25.1 us
  Pallas kernels  24.1 us (96%)
  local copies, waits for them, and re-layouts  0.97 us (4%)
    pallas_call x1, Pallas kernels, per_device(): pl.pallas_call(functools.partial(kernel, n), out_shape=pltpu.VMEM(excitat...  24.1 us
    unnamed x1, local copies, waits for them, and re-layouts  0.97 us

profile of v3, /device:TPU:6, one launch (start us, length us, event | category | flops | bytes accessed | tf_op | source)
XLA Modules:
  0.0 25.1 jit_solution(6714906568316177670)
XLA Ops:
  0.0 24.1 %shard_map.73 = f32[2,512,256]{2,1,0:T(8,128)S(1)} custom-call(f32[2,512,256]{2,1,0:T(8,128)} %x_hbm.1, bf16[2,256,512]{2,1,0:T(8,128)(2,1)} %leaf_hbm.1, bf16[3,2,256,256]{3,2,1,0:T(8,128)(2,1)} %self_hbm.1, bf16[3,2,256,256]{3,2,1,0:T(8,128)(2,1)} %cross_hbm.1, bf16[2,512,256]{2,1,0:T(8,128)(2,1)} %out_hbm.1, bf16[6,2,128,128]{3,2,1,0:T(8,128)(2,1)} %tiles_hbm.1, ...), custom_call_target="tpu_custom_call" | custom-call | tf_op jit(solution)/shard_map/pallas_call | solution.py:279
  24.1 1.0 %copy.9 = f32[2,512,256]{2,1,0:T(8,128)} copy(f32[2,512,256]{2,1,0:T(8,128)S(1)} %shard_map.73) | data formatting | bytes 2097152

commit v4 on v3

--- a/solution.py
+++ b/solution.py
@@ -8,7 +8,7 @@
 from jax.sharding import PartitionSpec as P
 
 MESH = pl.DeviceIdType.MESH
-CHUNKS = 2
+CUTS = (0, 128, 192, 256)
 SHEET = 128
 
 
@@ -44,8 +44,6 @@
     listed,
     near_send,
     near_recv,
-    coef,
-    got,
     terms,
     near,
     load_sem,
@@ -54,12 +52,14 @@
     send_sem,
     recv_sem,
     ready,
+    *traded,
 ):
     me = lax.axis_index("surf")
     levels = own.shape[0]
     blocks, tile, wide = xb.shape
     width = wide // 2
-    part = width // CHUNKS
+    chunks = len(CUTS) - 1
+    coef, got = traded[:chunks], traded[chunks:]
     slots = tiles.shape[0]
     group = 1 << levels
 
@@ -98,9 +98,23 @@
         loads[name] = pltpu.make_async_copy(src, dst, load_sem.at[len(loads)])
         loads[name].start()
 
-    load("x", x_hbm, xf)
+    for b in range(blocks):
+        rows = pl.ds(b * tile, tile)
+        load(f"x{b}", x_hbm.at[:, rows], xf.at[:, rows])
+    load("list", list_hbm, listed)
     load("leaf", leaf_hbm, leaf)
-    load("list", list_hbm, listed)
+
+    def until_ready(level):
+        @pl.when(jnp.logical_not(hub))
+        def _():
+            pl.semaphore_wait(ready.at[level], 1)
+
+    for b in range(blocks):
+        loads[f"x{b}"].wait()
+        rows = slice(b * tile, (b + 1) * tile)
+        both = jnp.concatenate([xf[0, rows, :], xf[1, rows, :]], axis=1).astype(jnp.bfloat16)
+        xb[b] = both
+
     for l in range(levels):
         load(f"self{l}", self_hbm.at[l], own.at[l])
         load(f"cross{l}", cross_hbm.at[l], cross.at[l])
@@ -128,29 +142,17 @@
     def _():
         answer(beside, last_side)
 
-    def until_ready(level):
-        @pl.when(jnp.logical_not(hub))
-        def _():
-            pl.semaphore_wait(ready.at[level], 1)
-
-    loads["x"].wait()
-    for b in range(blocks):
-        rows = slice(b * tile, (b + 1) * tile)
-        both = jnp.concatenate([xf[0, rows, :], xf[1, rows, :]], axis=1).astype(jnp.bfloat16)
-        xb[b] = both
-        window[b] = both
-
     def chunk(c):
-        lo, hi = c * part, (c + 1) * part
+        lo, hi = CUTS[c], CUTS[c + 1]
         rows = blocks * tile
-        real = xb[:, :, lo:hi].reshape(rows, part)
-        imag = xb[:, :, width + lo : width + hi].reshape(rows, part)
+        real = xb[:, :, lo:hi].reshape(rows, hi - lo)
+        imag = xb[:, :, width + lo : width + hi].reshape(rows, hi - lo)
         return jnp.concatenate([real, imag], axis=1)
 
     def exchange(level, c):
         return pltpu.make_async_remote_copy(
-            src_ref=coef.at[level, c],
-            dst_ref=got.at[level, c],
+            src_ref=coef[c].at[level],
+            dst_ref=got[c].at[level],
             send_sem=send_sem.at[level, c],
             recv_sem=recv_sem.at[level, c],
             device_id=(me ^ (1 << level),),
@@ -200,8 +202,8 @@
 
     loads["leaf"].wait()
     copies = {}
-    for c in range(CHUNKS):
-        coef[0, c] = cmul(leaf[0], leaf[1], chunk(c)).astype(jnp.bfloat16)
+    for c in range(chunks):
+        coef[c][0] = cmul(leaf[0], leaf[1], chunk(c)).astype(jnp.bfloat16)
         copies[0, c] = exchange(0, c)
         if c == 0:
             until_ready(0)
@@ -213,6 +215,8 @@
         loads["tiles"].wait()
         for copy in near_copies:
             copy.wait_recv()
+        for b in range(blocks):
+            window[b] = xb[b]
         for s in range(2):
             for h in range(2):
                 window[blocks + 2 * s + h] = near_recv[s, h]
@@ -236,16 +240,16 @@
 
     for l in range(levels):
         loads[f"self{l}"].wait()
-        sums = [cmul(own[l, 0], own[l, 1], coef[l, c]) for c in range(CHUNKS)]
+        sums = [cmul(own[l, 0], own[l, 1], coef[c][l]) for c in range(chunks)]
         if l + 1 == levels:
             send_beside(edge)
             near_field()
         loads[f"cross{l}"].wait()
-        for c in range(CHUNKS):
+        for c in range(chunks):
             copies[l, c].wait_recv()
-            after = (sums[c] + cmul(cross[l, 0], cross[l, 1], got[l, c])).astype(jnp.bfloat16)
+            after = (sums[c] + cmul(cross[l, 0], cross[l, 1], got[c][l])).astype(jnp.bfloat16)
             if l + 1 < levels:
-                coef[l + 1, c] = after
+                coef[c][l + 1] = after
                 copies[l + 1, c] = exchange(l + 1, c)
                 if c == 0:
                     until_ready(l + 1)
@@ -254,7 +258,8 @@
             if c == 0:
                 loads["out"].wait()
             far = cmul(outb[0], outb[1], after)
-            lo, hi = c * part, (c + 1) * part
+            lo, hi = CUTS[c], CUTS[c + 1]
+            part = hi - lo
             o_ref[0, :, lo:hi] = far[:, :part] + near[:, lo:hi]
             o_ref[1, :, lo:hi] = far[:, part:] + near[:, width + lo : width + hi]
     for copy in near_copies:
@@ -275,7 +280,9 @@
     by_slot = jnp.transpose(near_list, (1, 2, 0))
     half, full = jnp.bfloat16, jnp.float32
     anywhere = pl.BlockSpec(memory_space=pl.ANY)
-    part = 2 * width // CHUNKS
+    traded = [
+        pltpu.VMEM((levels, rank, 2 * (hi - lo)), half) for lo, hi in zip(CUTS, CUTS[1:])
+    ]
     return pl.pallas_call(
         functools.partial(kernel, n),
         out_shape=pltpu.VMEM(excitation.shape, full),
@@ -293,16 +300,16 @@
             pltpu.SMEM(by_slot.shape, jnp.int32),
             pltpu.VMEM((2, 2, tile, 2 * width), half),
             pltpu.VMEM((2, 2, tile, 2 * width), half),
-            pltpu.VMEM((levels, CHUNKS, rank, part), half),
-            pltpu.VMEM((levels, CHUNKS, rank, part), half),
             pltpu.VMEM((slots, tile, 2 * width), full),
             pltpu.VMEM((rows, 2 * width), full),
-            pltpu.SemaphoreType.DMA((5 + 2 * levels,)),
+            pltpu.SemaphoreType.DMA((4 + blocks + 2 * levels,)),
             pltpu.SemaphoreType.DMA((2,)),
             pltpu.SemaphoreType.DMA((2,)),
-            pltpu.SemaphoreType.DMA((levels, CHUNKS)),
-            pltpu.SemaphoreType.DMA((levels, CHUNKS)),
+            pltpu.SemaphoreType.DMA((levels, len(traded))),
+            pltpu.SemaphoreType.DMA((levels, len(traded))),
             pltpu.SemaphoreType.REGULAR((levels + 1,)),
+            *traded,
+            *traded,
         ],
         compiler_params=pltpu.CompilerParams(
             collective_id=0, has_side_effects=True, vmem_limit_bytes=24 << 20

time: 25.2 us -> 25.3 us (level)
  no operation moved by 1% of the time
where the time goes in v4:
time: 25.3 us; the launch traced here: 25.1 us
  Pallas kernels  24.2 us (96%)
  local copies, waits for them, and re-layouts  0.97 us (4%)
    pallas_call x1, Pallas kernels, per_device(): pl.pallas_call(functools.partial(kernel, n), out_shape=pltpu.VMEM(excitat...  24.2 us
    unnamed x1, local copies, waits for them, and re-layouts  0.97 us

profile of v4, /device:TPU:6, one launch (start us, length us, event | category | flops | bytes accessed | tf_op | source)
XLA Modules:
  0.0 25.1 jit_solution(12586373462117284479)
XLA Ops:
  0.0 24.2 %shard_map.73 = f32[2,512,256]{2,1,0:T(8,128)S(1)} custom-call(f32[2,512,256]{2,1,0:T(8,128)} %x_hbm.1, bf16[2,256,512]{2,1,0:T(8,128)(2,1)} %leaf_hbm.1, bf16[3,2,256,256]{3,2,1,0:T(8,128)(2,1)} %self_hbm.1, bf16[3,2,256,256]{3,2,1,0:T(8,128)(2,1)} %cross_hbm.1, bf16[2,512,256]{2,1,0:T(8,128)(2,1)} %out_hbm.1, bf16[6,2,128,128]{3,2,1,0:T(8,128)(2,1)} %tiles_hbm.1, ...), custom_call_target="tpu_custom_call" | custom-call | tf_op jit(solution)/shard_map/pallas_call | solution.py:286
  24.2 1.0 %copy.9 = f32[2,512,256]{2,1,0:T(8,128)} copy(f32[2,512,256]{2,1,0:T(8,128)S(1)} %shard_map.73) | data formatting | bytes 2097152
